TPU v7x, 32 devices: a whole 2x2x4 slice. The times are simulated.
32 devices in a mesh: groups: 2 (over y), chol: 4 (over z), occ: 4 (over x, core).
Axes of the slice: x: 2, y: 2, z: 4, core: 2. Of those that a mesh axis runs over, the one named last changes fastest.
Arguments:
- chol_rot: bfloat16 [96, 256, 2048], P(('groups', 'chol'), 'occ'), parts along dimension 0, may hold values from -0.1875 to 0.1875
- green: bfloat16 [4, 256, 2048], P('groups', 'occ', 'chol'), parts along dimension 0, may hold values from -6 to 6
Outputs:
- gradient: float32 [256, 4, 2048], P('occ', 'groups', 'chol'), parts along dimension 1
There are 2 independent parts, one for each index of `groups`. A program takes and returns all parts, laid end to end along the dimension named above; each array names one. Nothing has to cross between parts.
All inputs are finite; a program needn't handle non-finite values.
Results may differ from a plain program's by a relative error of at most 0.0085.
Values may be sent and summed in bfloat16 or wider, within the bound.
No kernel may reach another device: no remote copies, remote signals or barrier semaphores. Data moves between devices by JAX's collectives and lax.ppermute only.
A program may use at most 64 MiB of HBM per device.

v0:
```python
import math
import jax
import jax.numpy as jnp
from jax import lax
from jax.sharding import PartitionSpec as P


def local(chol_rot, green):
    chol_loc, occ_loc, orbitals = chol_rot.shape
    walkers = green.shape[0]
    occupied = occ_loc * lax.axis_size("occ")
    nvec = chol_loc * lax.axis_size("chol")
    factor = -math.sqrt(orbitals / (nvec * occupied))
    vec_mat = chol_rot.reshape(chol_loc * occ_loc, orbitals)
    green_all = lax.all_gather(green, "occ", axis=1, tiled=True)
    piece = lax.all_gather(green_all, "chol", axis=2, tiled=True)
    flat = piece.reshape(-1, piece.shape[2])
    pair_sum = jnp.dot(vec_mat, flat.T, preferred_element_type=jnp.float32)
    pairs = pair_sum.astype(jnp.bfloat16).reshape(chol_loc, occ_loc, walkers, occupied)
    swapped = lax.all_to_all(pairs, "occ", split_axis=3, concat_axis=1, tiled=True)
    occ_summed = lax.psum_scatter(
        jnp.einsum("gjwi,gip->jwp", swapped, chol_rot, preferred_element_type=jnp.float32).astype(
            jnp.bfloat16
        ),
        "occ",
        scatter_dimension=0,
        tiled=True,
    ).astype(jnp.float32)
    summed = lax.psum_scatter(occ_summed, "chol", scatter_dimension=2, tiled=True)
    return summed * factor


def solution(mesh):
    return jax.shard_map(
        local,
        mesh=mesh,
        in_specs=(P(("groups", "chol"), "occ", None), P("groups", "occ", "chol")),
        out_specs=P("occ", "groups", "chol"),
        check_vma=False,
    )
```

profile of v0, /device:TPU:0, one launch (start us, length us, event | category | flops | bytes accessed | tf_op | source)
XLA Modules:
  0.0 178.3 jit_solution(8074986663680790082)
XLA Ops:
  6.5 0.0 copy-start
  6.5 0.0 all-gather.2.cloned.1.call-start
  6.5 10.5 %all_gather.6 = bf16[2,256,512]{2,1,0:T(8,128)(2,1)} all-gather(bf16[2,64,512]{2,1,0:T(8,128)(2,1)} %param.3), channel_id=1, replica_groups=mesh['groups'=2,'chol'=4,'occ'=4] {'occ'}, dimensions={1}, use_global_device_ids=true | all-gather | bytes 655360 | tf_op jit(solution)/shard_map/all_gather | solution.py:15
  17.0 0.0 all-gather.2.cloned.1.call-update
  17.0 0.0 reduce-scatter.3.cloned.1.call-start
  17.1 46.1 %all-gather.2.cloned.1.call-done = bf16[2,256,2048]{2,1,0:T(8,128)(2,1)} async-done(((bf16[2,256,512]{2,1,0:T(8,128)(2,1)}), bf16[2,256,2048]{2,1,0:T(8,128)(2,1)}) %all-gather.2.cloned.1.call-update) | async-done | bytes 2097168 | tf_op jit(solution)/shard_map/all_gather | solution.py:16
  63.2 0.0 copy-done
  63.2 4.3 %convolution_convert_fusion = bf16[768,512]{1,0:T(8,128)(2,1)} fusion(bf16[768,2048]{1,0:T(8,128)(2,1)S(1)} %bitcast.19, bf16[512,2048]{1,0:T(8,128)(2,1)} %bitcast.23), kind=kOutput, calls=%fused_computation.3 | convolution fusion | flops 1611005952 | bytes 6029312 | tf_op jit(solution)/shard_map/dot_general | solution.py:18
  67.5 2.9 %reshape.11 = bf16[12,64,2,256]{3,2,1,0:T(2,128)(2,1)} reshape(bf16[768,512]{1,0:T(8,128)(2,1)} %convolution_convert_fusion) | data formatting | bytes 1572864 | tf_op jit(solution)/shard_map/reshape | solution.py:19
  70.4 5.0 %copy.8 = bf16[12,64,2,256]{1,2,0,3:T(2,128)(2,1)} copy(bf16[12,64,2,256]{3,2,1,0:T(2,128)(2,1)} %reshape.11) | data formatting | bytes 1572864 | tf_op jit(solution)/shard_map/reshape | solution.py:19
  75.4 4.0 %reshape.14 = bf16[4,2,49152]{2,1,0:T(2,128)(2,1)} reshape(bf16[256,12,2,64]{3,2,1,0:T(2,128)(2,1)} %bitcast.20) | data formatting | bytes 1572864
  79.5 15.9 %all_to_all.18 = bf16[4,2,49152]{2,1,0:T(2,128)(2,1)} all-to-all(bf16[4,2,49152]{2,1,0:T(2,128)(2,1)} %reshape.14), channel_id=1, replica_groups=mesh['groups'=2,'chol'=4,'occ'=4] {'occ'}, dimensions={0} | all-to-all | bytes 1572864 | tf_op jit(solution)/shard_map/all_to_all | solution.py:20
  95.4 4.0 %reshape.15 = bf16[256,12,2,64]{3,2,1,0:T(2,128)(2,1)} reshape(bf16[4,2,49152]{2,1,0:T(2,128)(2,1)} %all_to_all.18) | data formatting | bytes 1572864
  99.3 3.8 %copy.13 = bf16[12,64,2,4,64]{1,3,4,0,2:T(4,128)(2,1)} copy(bf16[12,64,2,4,64]{1,2,0,4,3:T(2,128)(2,1)} %bitcast.21) | data formatting | bytes 1572864 | tf_op jit(solution)/shard_map/all_to_all | solution.py:20
  103.1 3.6 %all_to_all.16 = bf16[12,256,2,64]{1,3,0,2:T(8,128)(2,1)} reshape(bf16[12,4,64,2,64]{2,1,4,0,3:T(4,128)(2,1)} %bitcast.22) | data formatting | bytes 1572864 | tf_op jit(solution)/shard_map/all_to_all | solution.py:20
  106.7 4.3 %bitcast_convert_fusion = bf16[256,2,2048]{2,0,1:T(8,128)(2,1)} fusion(bf16[12,256,2,64]{1,3,0,2:T(8,128)(2,1)} %all_to_all.16, bf16[12,64,2048]{2,1,0:T(8,128)(2,1)S(1)} %copy-done), kind=kOutput, calls=%fused_computation | convolution fusion | flops 1611661312 | bytes 6029312 | tf_op jit(solution)/shard_map/gjwi,gip->jwp/dot_general | solution.py:22
  111.0 0.0 reduce-scatter.3.cloned.1.call-update
  111.0 0.0 reduce-scatter.5.cloned.1.call-start
  111.1 29.2 %reduce-scatter.3.cloned.1.call-done = bf16[64,2,2048]{2,0,1:T(8,128)(2,1)} async-done(((bf16[256,2,2048]{2,0,1:T(8,128)(2,1)}), bf16[64,2,2048]{2,0,1:T(8,128)(2,1)}) %reduce-scatter.3.cloned.1.call-update) | async-done | bytes 524304 | tf_op jit(solution)/shard_map/reduce_scatter | solution.py:21
  140.2 2.1 %convert_element_type.11 = f32[64,2,2048]{2,0,1:T(8,128)} convert(bf16[64,2,2048]{2,0,1:T(8,128)(2,1)} %reduce-scatter.3.cloned.1.call-done) | non-fusion elementwise | flops 262144 | bytes 1572864 | tf_op jit(solution)/shard_map/convert_element_type | solution.py:28
  142.3 0.0 reduce-scatter.5.cloned.1.call-update
  142.4 27.5 %reduce-scatter.5.cloned.1.call-done = f32[64,2,512]{2,0,1:T(8,128)} async-done(((f32[64,2,2048]{2,0,1:T(8,128)}), f32[64,2,512]{2,0,1:T(8,128)}) %reduce-scatter.5.cloned.1.call-update) | async-done | bytes 262160 | tf_op jit(solution)/shard_map/reduce_scatter | solution.py:29
  169.9 1.0 broadcast_multiply_fusion
  170.8 0.9 copy.10
Async XLA Ops:
  6.5 56.6 %copy-start = (bf16[12,64,2048]{2,1,0:T(8,128)(2,1)S(1)}, bf16[12,64,2048]{2,1,0:T(8,128)(2,1)}, u32[]{:S(2)}) copy-start(bf16[12,64,2048]{2,1,0:T(8,128)(2,1)} %param.2) | copy-start | bytes 9437188
  6.5 56.6 %all-gather.2.cloned.1.call-start = ((), (), s32[]{:S(2)}) async-start(), calls=%async_computation.3 | async-start | bytes 2621440 | tf_op jit(solution)/shard_map/all_gather | solution.py:16
  17.0 123.2 %reduce-scatter.3.cloned.1.call-start = ((), (), s32[]{:S(2)}) async-start(), calls=%async_computation.4 | async-start | bytes 2621440 | tf_op jit(solution)/shard_map/reduce_scatter | solution.py:21
  111.0 58.9 %reduce-scatter.5.cloned.1.call-start = ((), (), s32[]{:S(2)}) async-start(), calls=%async_computation.5 | async-start | bytes 1310720 | tf_op jit(solution)/shard_map/reduce_scatter | solution.py:29
Sparse Core Ops, SparseCore 0:
  17.2 45.9 all-gather.1
  111.1 29.0 reduce-scatter.2
  142.5 27.3 reduce-scatter.4
where the time goes:
time: 179 us; the launch traced here: 178 us
  waiting for transfers between devices  103 us (58%)
  blocking collectives  26.4 us (15%)
  local copies, waits for them, and re-layouts  24.2 us (14%)
  between operations  13.1 us (7%)
  matrix products  8.59 us (5%)
  other arithmetic  3.09 us (2%)
    all_gather x1, waiting for transfers between devices, local(): piece = lax.all_gather(green_all, 'chol', axis=2, tiled=True)  46.1 us
    reduce_scatter x1, waiting for transfers between devices, local(): lax.psum_scatter(jnp.einsum('gjwi,gip->jwp', swapped, chol_rot, preferred...  29.2 us
    reduce_scatter x1, waiting for transfers between devices, local(): lax.psum_scatter(occ_summed, 'chol', scatter_dimension=2, tiled=True)  27.5 us
    all_to_all x1, blocking collectives, local(): lax.all_to_all(pairs, 'occ', split_axis=3, concat_axis=1, tiled=True)  15.9 us
    all_gather x1, blocking collectives, local(): green_all = lax.all_gather(green, 'occ', axis=1, tiled=True)  10.5 us
    unnamed x4, local copies, waits for them, and re-layouts  8.02 us
    reshape x2, local copies, waits for them, and re-layouts, local(): pair_sum.astype(jnp.bfloat16).reshape(chol_loc, occ_loc, walkers, occupied)  7.95 us
    all_to_all x2, local copies, waits for them, and re-layouts, local(): lax.all_to_all(pairs, 'occ', split_axis=3, concat_axis=1, tiled=True)  7.37 us
  transfers between devices with their start and end apart: 3, of which 3 were waited for; matrix products, arithmetic and copies ran while one was open for 0% of the time, Pallas kernels for 0%

commit v1 on v0

--- a/solution.py
+++ b/solution.py
@@ -17,7 +17,10 @@
     flat = piece.reshape(-1, piece.shape[2])
     pair_sum = jnp.dot(vec_mat, flat.T, preferred_element_type=jnp.float32)
     pairs = pair_sum.astype(jnp.bfloat16).reshape(chol_loc, occ_loc, walkers, occupied)
-    swapped = lax.all_to_all(pairs, "occ", split_axis=3, concat_axis=1, tiled=True)
+    swapped = jnp.concatenate(
+        lax.all_to_all(jnp.stack(jnp.split(pairs, lax.axis_size("occ"), axis=3)), "occ", 0, 0),
+        axis=1,
+    )
     occ_summed = lax.psum_scatter(
         jnp.einsum("gjwi,gip->jwp", swapped, chol_rot, preferred_element_type=jnp.float32).astype(
             jnp.bfloat16

time: 179 us -> 182 us (1.017)
  other arithmetic: 3.09 us -> 7.11 us
    reshape x0 -> x2, local copies, waits for them, and re-layouts: none -> 8.73 us  [local(): jnp.concatenate(lax.all_to_all(jnp.stack(jnp.split(pairs, lax.axis_size('...]
    all_to_all x2 -> x0, local copies, waits for them, and re-layouts: 7.37 us -> none  [local(): lax.all_to_all(pairs, 'occ', split_axis=3, concat_axis=1, tiled=True)]
    reshape x2 -> x1, local copies, waits for them, and re-layouts: 7.95 us -> 2.9 us  [local(): pair_sum.astype(jnp.bfloat16).reshape(chol_loc, occ_loc, walkers, occupied)]
    another operation x0 -> x1, other arithmetic: none -> 4.01 us  [local(): jnp.stack(jnp.split(pairs, lax.axis_size('occ'), axis=3))]
    another operation x0 -> x1, local copies, waits for them, and re-layouts: none -> 2.91 us  [local(): jnp.stack(jnp.split(pairs, lax.axis_size('occ'), axis=3))]
where the time goes in v1:
time: 182 us
  waiting for transfers between devices  103 us (57%)
  blocking collectives  26.4 us (15%)
  local copies, waits for them, and re-layouts  23.4 us (13%)
  between operations  13.1 us (7%)
  matrix products  8.6 us (5%)
  other arithmetic  7.11 us (4%)
    all_gather x1, waiting for transfers between devices, local(): piece = lax.all_gather(green_all, 'chol', axis=2, tiled=True)  46.1 us
    reduce_scatter x1, waiting for transfers between devices, local(): lax.psum_scatter(jnp.einsum('gjwi,gip->jwp', swapped, chol_rot, preferred...  29.2 us
    reduce_scatter x1, waiting for transfers between devices, local(): lax.psum_scatter(occ_summed, 'chol', scatter_dimension=2, tiled=True)  27.5 us
    all_to_all x1, blocking collectives, local(): lax.all_to_all(jnp.stack(jnp.split(pairs, lax.axis_size('occ'), axis=3)),...  15.9 us
    all_gather x1, blocking collectives, local(): green_all = lax.all_gather(green, 'occ', axis=1, tiled=True)  10.5 us
    reshape x2, local copies, waits for them, and re-layouts, local(): jnp.concatenate(lax.all_to_all(jnp.stack(jnp.split(pairs, lax.axis_size('...  8.73 us
    unnamed x4, local copies, waits for them, and re-layouts  8 us
    dot_general x1, matrix products, local(): pair_sum = jnp.dot(vec_mat, flat.T, preferred_element_type=jnp.float32)  4.3 us
  transfers between devices with their start and end apart: 3, of which 3 were waited for; matrix products, arithmetic and copies ran while one was open for 0% of the time, Pallas kernels for 0%

profile of v1, /device:TPU:0, one launch (start us, length us, event | category | flops | bytes accessed | tf_op | source)
XLA Modules:
  0.0 181.5 jit_solution(2749192723687867755)
XLA Ops:
  6.5 0.0 copy-start
  6.5 0.0 all-gather.2.cloned.1.call-start
  6.5 10.5 %all_gather.6 = bf16[2,256,512]{2,1,0:T(8,128)(2,1)} all-gather(bf16[2,64,512]{2,1,0:T(8,128)(2,1)} %param.3), channel_id=1, replica_groups=mesh['groups'=2,'chol'=4,'occ'=4] {'occ'}, dimensions={1}, use_global_device_ids=true | all-gather | bytes 655360 | tf_op jit(solution)/shard_map/all_gather | solution.py:15
  17.0 0.0 all-gather.2.cloned.1.call-update
  17.0 0.0 reduce-scatter.3.cloned.1.call-start
  17.1 46.1 %all-gather.2.cloned.1.call-done = bf16[2,256,2048]{2,1,0:T(8,128)(2,1)} async-done(((bf16[2,256,512]{2,1,0:T(8,128)(2,1)}), bf16[2,256,2048]{2,1,0:T(8,128)(2,1)}) %all-gather.2.cloned.1.call-update) | async-done | bytes 2097168 | tf_op jit(solution)/shard_map/all_gather | solution.py:16
  63.2 0.0 copy-done
  63.2 4.3 %convolution_convert_fusion = bf16[768,512]{1,0:T(8,128)(2,1)} fusion(bf16[768,2048]{1,0:T(8,128)(2,1)S(1)} %bitcast.22, bf16[512,2048]{1,0:T(8,128)(2,1)} %bitcast.24), kind=kOutput, calls=%fused_computation.3 | convolution fusion | flops 1611005952 | bytes 6029312 | tf_op jit(solution)/shard_map/dot_general | solution.py:18
  67.5 2.9 %reshape.17 = bf16[12,64,2,256]{3,2,1,0:T(2,128)(2,1)} reshape(bf16[768,512]{1,0:T(8,128)(2,1)} %convolution_convert_fusion) | data formatting | bytes 1572864 | tf_op jit(solution)/shard_map/reshape | solution.py:19
  70.4 2.9 %slice_bitcast_fusion.3 = (bf16[1,12,64,2,64]{4,3,2,1,0:T(2,128)(2,1)S(1)}, bf16[1,12,64,2,64]{4,3,2,1,0:T(2,128)(2,1)S(1)}, bf16[1,12,64,2,64]{4,3,2,1,0:T(2,128)(2,1)S(1)}, bf16[1,12,64,2,64]{4,3,2,1,0:T(2,128)(2,1)S(1)}) fusion(bf16[12,64,2,256]{3,2,1,0:T(2,128)(2,1)} %reshape.17), kind=kLoop, calls=%fused_computation.7 | loop fusion | bytes 1572864 | tf_op jit(solution)/shard_map/stack | solution.py:21
  73.3 4.0 %pad_maximum_fusion = bf16[4,12,64,2,64]{4,3,2,1,0:T(2,128)(2,1)} fusion(bf16[1,12,64,2,64]{4,3,2,1,0:T(2,128)(2,1)S(1)} %get-tuple-element.6, bf16[1,12,64,2,64]{4,3,2,1,0:T(2,128)(2,1)S(1)} %get-tuple-element.7, bf16[1,12,64,2,64]{4,3,2,1,0:T(2,128)(2,1)S(1)} %get-tuple-element.8, bf16[1,12,64,2,64]{4,3,2,1,0:T(2,128)(2,1)S(1)} %get-tuple-element.5), kind=kLoop, calls=%fused_computation.2 | loop fusion | flops 1179648 | bytes 1572864 | tf_op jit(solution)/shard_map/stack | solution.py:21
  77.3 4.0 %reshape.22 = bf16[4,2,49152]{2,1,0:T(2,128)(2,1)} reshape(bf16[4,12,64,2,64]{4,3,2,1,0:T(2,128)(2,1)} %pad_maximum_fusion) | data formatting | bytes 1572864
  81.3 15.9 %all_to_all.5 = bf16[4,2,49152]{2,1,0:T(2,128)(2,1)} all-to-all(bf16[4,2,49152]{2,1,0:T(2,128)(2,1)} %reshape.22), channel_id=1, replica_groups=mesh['groups'=2,'chol'=4,'occ'=4] {'occ'}, dimensions={0} | all-to-all | bytes 1572864 | tf_op jit(solution)/shard_map/all_to_all | solution.py:21
  97.2 4.0 %reshape.23 = bf16[4,12,64,2,64]{4,3,2,1,0:T(2,128)(2,1)} reshape(bf16[4,2,49152]{2,1,0:T(2,128)(2,1)} %all_to_all.5) | data formatting | bytes 1572864
  101.2 5.1 %copy.3 = bf16[12,4,64,2,64]{2,1,4,0,3:T(4,128)(2,1)} copy(bf16[12,4,64,2,64]{4,3,2,0,1:T(2,128)(2,1)} %bitcast.23) | data formatting | bytes 1572864 | tf_op jit(solution)/shard_map/reshape | solution.py:20
  106.3 3.6 %reshape.19 = bf16[12,256,2,64]{1,3,0,2:T(8,128)(2,1)} reshape(bf16[12,4,64,2,64]{2,1,4,0,3:T(4,128)(2,1)} %copy.3) | data formatting | bytes 1572864 | tf_op jit(solution)/shard_map/reshape | solution.py:20
  109.9 4.3 %bitcast_convert_fusion = bf16[256,2,2048]{2,0,1:T(8,128)(2,1)} fusion(bf16[12,256,2,64]{1,3,0,2:T(8,128)(2,1)} %reshape.19, bf16[12,64,2048]{2,1,0:T(8,128)(2,1)S(1)} %copy-done), kind=kOutput, calls=%fused_computation | convolution fusion | flops 1611661312 | bytes 6029312 | tf_op jit(solution)/shard_map/gjwi,gip->jwp/dot_general | solution.py:25
  114.2 0.0 reduce-scatter.3.cloned.1.call-update
  114.2 0.0 reduce-scatter.5.cloned.1.call-start
  114.3 29.2 %reduce-scatter.3.cloned.1.call-done = bf16[64,2,2048]{2,0,1:T(8,128)(2,1)} async-done(((bf16[256,2,2048]{2,0,1:T(8,128)(2,1)}), bf16[64,2,2048]{2,0,1:T(8,128)(2,1)}) %reduce-scatter.3.cloned.1.call-update) | async-done | bytes 524304 | tf_op jit(solution)/shard_map/reduce_scatter | solution.py:24
  143.5 2.1 %convert_element_type.11 = f32[64,2,2048]{2,0,1:T(8,128)} convert(bf16[64,2,2048]{2,0,1:T(8,128)(2,1)} %reduce-scatter.3.cloned.1.call-done) | non-fusion elementwise | flops 262144 | bytes 1572864 | tf_op jit(solution)/shard_map/convert_element_type | solution.py:31
  145.6 0.0 reduce-scatter.5.cloned.1.call-update
  145.6 27.5 %reduce-scatter.5.cloned.1.call-done = f32[64,2,512]{2,0,1:T(8,128)} async-done(((f32[64,2,2048]{2,0,1:T(8,128)}), f32[64,2,512]{2,0,1:T(8,128)}) %reduce-scatter.5.cloned.1.call-update) | async-done | bytes 262160 | tf_op jit(solution)/shard_map/reduce_scatter | solution.py:32
  173.1 1.0 broadcast_multiply_fusion
  174.1 0.9 copy.4
Async XLA Ops:
  6.5 56.6 %copy-start = (bf16[12,64,2048]{2,1,0:T(8,128)(2,1)S(1)}, bf16[12,64,2048]{2,1,0:T(8,128)(2,1)}, u32[]{:S(2)}) copy-start(bf16[12,64,2048]{2,1,0:T(8,128)(2,1)} %param.2) | copy-start | bytes 9437188
  6.5 56.6 %all-gather.2.cloned.1.call-start = ((), (), s32[]{:S(2)}) async-start(), calls=%async_computation.3 | async-start | bytes 2621440 | tf_op jit(solution)/shard_map/all_gather | solution.py:16
  17.0 126.4 %reduce-scatter.3.cloned.1.call-start = ((), (), s32[]{:S(2)}) async-start(), calls=%async_computation.4 | async-start | bytes 2621440 | tf_op jit(solution)/shard_map/reduce_scatter | solution.py:24
  114.2 58.9 %reduce-scatter.5.cloned.1.call-start = ((), (), s32[]{:S(2)}) async-start(), calls=%async_computation.5 | async-start | bytes 1310720 | tf_op jit(solution)/shard_map/reduce_scatter | solution.py:32
Sparse Core Ops, SparseCore 0:
  17.2 45.9 all-gather.1
  114.4 29.0 reduce-scatter.2
  145.7 27.3 reduce-scatter.4
